TPU v7x, 256 devices: a whole 4x4x8 slice. The times are simulated.
256 devices in a mesh: rows: 8 (over x, core), protos: 32 (over y, z).
Axes of the slice: x: 4, y: 4, z: 8, core: 2. Of those that a mesh axis runs over, the one named last changes fastest.
Arguments:
- teacher_features: bfloat16 [4096, 384], P(('rows', 'protos')), may hold values from -80 to 80, as said below
- student_features: bfloat16 [4096, 384], P(('rows', 'protos')), may hold values from -80 to 80, as said below
- prototypes: bfloat16 [131072, 384], P('protos'), may hold values from -80 to 80, as said below
Outputs:
- feature_grad: float32 [4096, 384], P(('rows', 'protos'))
- proto_grad: float32 [8, 16384, 384], P('rows', 'protos')
Inputs may be any that keep to these rules, and one draw needn't show every extreme that they name: `teacher_features`: every row has nonzero entries. `student_features`: every row has nonzero entries. `prototypes`: every row has nonzero entries.
All inputs are finite; a program needn't handle non-finite values.
Results may differ from a plain program's by a relative error of at most 0.012.
The roundings to bfloat16 on the way count: a program that leaves them out, or rounds other values in their place, can miss the bound.
Values may be sent and summed in bfloat16 or wider, within the bound.
A program may use at most 64 MiB of HBM per device.

v0:
```python
import math
import jax
import jax.numpy as jnp
from jax import lax
from jax.sharding import PartitionSpec as P

D = 384
K = 131072
PASSES = 3
eps = 1e-06


def unitize(values):
    values = values.astype(jnp.float32)
    return (values * lax.rsqrt(jnp.sum(values * values, axis=1, keepdims=True) + eps)).astype(
        jnp.bfloat16
    )


def against(left, right):
    return lax.dot_general(
        left, right, (((1,), (1,)), ((), ())), preferred_element_type=jnp.float32
    )


def on_device(teacher_features, student_features, prototypes):
    scale = 1.5 * math.sqrt(D)
    unit_w = unitize(prototypes)
    local_t = unitize(teacher_features)
    local_s = unitize(student_features)
    unit_t, unit_s = (
        lax.all_gather(local_t, "protos", axis=0, tiled=True),
        lax.all_gather(local_s, "protos", axis=0, tiled=True),
    )
    kernel = jnp.exp(scale * against(unit_t, unit_w))
    powers = jnp.exp(scale * against(unit_s, unit_w))
    student_part = jnp.sum(powers, axis=1)
    student_whole = lax.psum(student_part, "protos")
    row_scale = jnp.ones((kernel.shape[0],), jnp.float32)
    col_scale = jnp.ones((kernel.shape[1],), jnp.float32)
    for step in range(PASSES):
        col_part = jnp.dot(row_scale, kernel, precision=lax.Precision.HIGHEST)
        col_scale = 1.0 / lax.psum(col_part, "rows")
        row_part = jnp.dot(kernel, col_scale, precision=lax.Precision.HIGHEST)
        if step == 0:
            row_whole = lax.psum(row_part, "protos")
        else:
            row_whole = lax.psum(row_part, "protos")
        row_scale = 1.0 / row_whole
    target = kernel * row_scale[:, None] * col_scale[None, :]
    probs = powers / student_whole[:, None]
    delta = (probs - target).astype(jnp.bfloat16)
    feature_term = scale * jnp.dot(delta, unit_w, preferred_element_type=jnp.float32)
    feature_grad = lax.psum_scatter(feature_term, "protos", scatter_dimension=0, tiled=True)
    row_groups = lax.axis_size("rows")
    total_rows = delta.shape[0] * row_groups
    factor = scale * K / total_rows
    block = delta.shape[1] // row_groups
    term = factor * lax.dot_general(
        delta, unit_s, (((0,), (0,)), ((), ())), preferred_element_type=jnp.float32
    )
    proto_grad = lax.psum_scatter(
        term.reshape(row_groups, block, term.shape[1]), "rows", scatter_dimension=0, tiled=True
    )
    return (feature_grad, proto_grad)


def solution(mesh):
    return jax.shard_map(
        on_device,
        mesh=mesh,
        in_specs=(P(("rows", "protos"), None), P(("rows", "protos"), None), P("protos", None)),
        out_specs=(P(("rows", "protos"), None), P("rows", "protos", None)),
        check_vma=False,
    )
```

profile of v0, /device:TPU:1, one launch (start us, length us, event | category | flops | bytes accessed | tf_op | source)
XLA Modules:
  0.0 735.6 jit_solution(5828482277272511359)
XLA Ops:
  7.2 0.0 reduce-scatter.3.cloned.1.call-start
  7.2 0.8 fusion.5
  8.0 0.8 fusion.3
  8.9 0.8 fusion.4
  9.7 0.8 fusion.6
  10.4 2.6 fusion.1
  13.0 0.0 copy-start.3
  13.1 41.6 %all_gather.6 = bf16[512,384]{1,0:T(8,128)(2,1)S(1)} all-gather(bf16[16,384]{1,0:T(8,128)(2,1)S(1)} %fusion.4), channel_id=1, replica_groups=mesh['rows'=8,'protos'=32] {'protos'}, dimensions={0}, use_global_device_ids=true | all-gather | bytes 405504 | tf_op jit(solution)/shard_map/all_gather | solution.py:33
  54.6 36.7 %all_gather.7 = bf16[512,384]{1,0:T(8,128)(2,1)S(1)} all-gather(bf16[16,384]{1,0:T(8,128)(2,1)S(1)} %fusion.6), channel_id=1, replica_groups=mesh['rows'=8,'protos'=32] {'protos'}, dimensions={0}, use_global_device_ids=true | all-gather | bytes 405504 | tf_op jit(solution)/shard_map/all_gather | solution.py:32
  91.3 4.3 multiply_exponential_fusion
  95.7 0.0 copy-start
  95.7 3.2 copy-done
  98.9 4.0 fusion.7
  102.9 0.0 copy-done.3
  102.9 44.7 %psum.50 = f32[4096]{0:T(1024)S(1)} all-reduce(f32[4096]{0:T(1024)S(1)} %bitcast.34), channel_id=1, replica_groups=mesh['rows'=8,'protos'=32] {'rows'}, use_global_device_ids=true, to_apply=%region_5.0 | all-reduce | flops 4096 | bytes 32768 | tf_op jit(solution)/shard_map/psum | solution.py:43
  147.7 9.4 %fusion.14 = f32[1,512]{1,0:T(1,128)S(1)} fusion(f32[512,4096]{1,0:T(8,128)} %copy-done, f32[4096,1]{0,1:T(1,128)S(1)} %bitcast.30), kind=kOutput, calls=%fused_computation.31 | convolution fusion | flops 25165824 | bytes 8407040 | tf_op jit(solution)/shard_map/dot_general | solution.py:44
  157.1 58.6 %psum.51 = f32[512]{0:T(512)S(1)} all-reduce(f32[512]{0:T(512)S(1)} %bitcast.36), channel_id=1, replica_groups=mesh['rows'=8,'protos'=32] {'protos'}, use_global_device_ids=true, to_apply=%region_6.0 | all-reduce | flops 512 | bytes 4096 | tf_op jit(solution)/shard_map/psum | solution.py:46
  215.7 6.3 fusion.15
  222.1 37.4 %psum.52 = f32[4096]{0:T(1024)S(1)} all-reduce(f32[4096]{0:T(1024)S(1)} %bitcast.31), channel_id=1, replica_groups=mesh['rows'=8,'protos'=32] {'rows'}, use_global_device_ids=true, to_apply=%region_7.0 | all-reduce | flops 4096 | bytes 32768 | tf_op jit(solution)/shard_map/psum | solution.py:43
  259.5 9.4 %fusion.16 = f32[1,512]{1,0:T(1,128)S(1)} fusion(f32[512,4096]{1,0:T(8,128)} %copy-done, f32[4096,1]{0,1:T(1,128)S(1)} %bitcast.32), kind=kOutput, calls=%fused_computation.33 | convolution fusion | flops 25165824 | bytes 8407040 | tf_op jit(solution)/shard_map/dot_general | solution.py:44
  268.9 55.8 %psum.53 = f32[512]{0:T(512)S(1)} all-reduce(f32[512]{0:T(512)S(1)} %bitcast.38), channel_id=1, replica_groups=mesh['rows'=8,'protos'=32] {'protos'}, use_global_device_ids=true, to_apply=%region_8.0 | all-reduce | flops 512 | bytes 4096 | tf_op jit(solution)/shard_map/psum | solution.py:48
  324.7 0.0 copy-start.1
  324.7 6.5 fusion.17
  331.2 37.6 %psum.54 = f32[4096]{0:T(1024)} all-reduce(f32[4096]{0:T(1024)S(1)} %bitcast.33), channel_id=1, replica_groups=mesh['rows'=8,'protos'=32] {'rows'}, use_global_device_ids=true, to_apply=%region_9.0 | all-reduce | flops 4096 | bytes 32768 | tf_op jit(solution)/shard_map/psum | solution.py:43
  368.8 0.7 broadcast_divide_fusion
  369.6 10.0 %fusion.18 = f32[1,512]{1,0:T(1,128)} fusion(f32[512,4096]{1,0:T(8,128)} %copy-done, f32[4096,1]{0,1:T(1,128)S(1)} %bitcast.29), kind=kOutput, calls=%fused_computation.35 | convolution fusion | flops 25165824 | bytes 8407040 | tf_op jit(solution)/shard_map/dot_general | solution.py:44
  379.6 0.0 copy-done.1
  379.6 6.2 fusion
  385.8 58.2 %all-reduce = (f32[512]{0:T(512)}, f32[512]{0:T(512)}) all-reduce(f32[512]{0:T(512)} %bitcast.35, f32[512]{0:T(512)} %get-tuple-element.4), channel_id=1, replica_groups=mesh['rows'=8,'protos'=32] {'protos'}, use_global_device_ids=true, to_apply=%region_10.0 | all-reduce | flops 1024 | bytes 8192 | tf_op jit(solution)/shard_map/psum | solution.py:48
  444.0 0.7 broadcast_divide_fusion.5
  444.6 0.0 copy-start.4
  444.6 7.3 subtract_convert_fusion
  452.0 0.0 copy-start.2
  452.0 2.0 copy-done.2
  454.0 0.0 copy-done.4
  454.0 3.3 convolution_multiply_fusion.1
  457.4 0.0 reduce-scatter.3.cloned.1.call-update
  457.4 0.0 reduce-scatter.5.cloned.1.call-start
  457.4 7.2 convolution_multiply_fusion
  464.7 0.0 reduce-scatter.5.cloned.1.call-update
  464.7 212.9 %reduce-scatter.3.cloned.1.call-done = f32[16,384]{1,0:T(8,128)} async-done(((f32[512,384]{1,0:T(8,128)}), f32[16,384]{1,0:T(8,128)}) %reduce-scatter.3.cloned.1.call-update) | async-done | bytes 24592 | tf_op jit(solution)/shard_map/reduce_scatter | solution.py:54
  677.6 51.2 %reduce-scatter.5.cloned.1.call-done = f32[1,512,384]{2,1,0:T(8,128)} async-done(((f32[8,512,384]{2,1,0:T(8,128)}), f32[1,512,384]{2,1,0:T(8,128)}) %reduce-scatter.5.cloned.1.call-update) | async-done | bytes 786448 | tf_op jit(solution)/shard_map/reduce_scatter | solution.py:62
  (7 shorter events, 0.0 us)
Async XLA Ops:
  7.2 670.4 %reduce-scatter.3.cloned.1.call-start = ((), (), s32[]{:S(2)}) async-start(), calls=%async_computation.2 | async-start | bytes 811008 | tf_op jit(solution)/shard_map/reduce_scatter | solution.py:54
  13.0 89.9 %copy-start.3 = (f32[4096]{0:T(1024)}, f32[4096]{0:T(1024)S(1)}, u32[]{:S(2)}) copy-start(f32[4096]{0:T(1024)S(1)} %add_rsqrt_fusion) | copy-start | bytes 49156
  95.7 3.2 copy-start
  324.7 54.9 %copy-start.1 = (bf16[4096,384]{1,0:T(8,128)(2,1)S(1)}, bf16[4096,384]{1,0:T(8,128)(2,1)}, u32[]{:S(2)}) copy-start(bf16[4096,384]{1,0:T(8,128)(2,1)} %param.5) | copy-start | bytes 9437188
  444.6 9.4 %copy-start.4 = (f32[4096]{0:T(1024)S(1)}, f32[4096]{0:T(1024)}, u32[]{:S(2)}) copy-start(f32[4096]{0:T(1024)} %copy-done.3) | copy-start | bytes 49156
  452.0 2.0 copy-start.2
  457.4 271.4 %reduce-scatter.5.cloned.1.call-start = ((), (), s32[]{:S(2)}) async-start(), calls=%async_computation.3 | async-start | bytes 7077888 | tf_op jit(solution)/shard_map/reduce_scatter | solution.py:62
Sparse Core Ops, SparseCore 0:
  457.5 220.0 reduce-scatter.2
  680.7 48.0 reduce-scatter.4
where the time goes:
time: 736 us
  blocking collectives  371 us (50%)
  waiting for transfers between devices  264 us (36%)
  matrix products  66.9 us (9%)
  other arithmetic  14.6 us (2%)
  between operations  14.1 us (2%)
    reduce_scatter x1, waiting for transfers between devices, on_device(): lax.psum_scatter(feature_term, 'protos', scatter_dimension=0, tiled=True)  213 us
    psum x3, blocking collectives, on_device(): row_whole = lax.psum(row_part, 'protos')  173 us
    psum x3, blocking collectives, on_device(): col_scale = 1.0 / lax.psum(col_part, 'rows')  120 us
    reduce_scatter x1, waiting for transfers between devices, on_device(): lax.psum_scatter(term.reshape(row_groups, block, term.shape[1]), 'rows',...  51.2 us
    all_gather x1, blocking collectives, on_device(): lax.all_gather(local_s, 'protos', axis=0, tiled=True)  41.6 us
    all_gather x1, blocking collectives, on_device(): lax.all_gather(local_t, 'protos', axis=0, tiled=True)  36.7 us
    dot_general x3, matrix products, on_device(): row_part = jnp.dot(kernel, col_scale, precision=lax.Precision.HIGHEST)  28.9 us
    dot_general x3, matrix products, on_device(): col_part = jnp.dot(row_scale, kernel, precision=lax.Precision.HIGHEST)  16.9 us
  transfers between devices with their start and end apart: 2, of which 2 were waited for; matrix products, arithmetic and copies ran while one was open for 1% of the time, Pallas kernels for 0%

commit v1 on v0

--- a/solution.py
+++ b/solution.py
@@ -43,7 +43,8 @@
         col_scale = 1.0 / lax.psum(col_part, "rows")
         row_part = jnp.dot(kernel, col_scale, precision=lax.Precision.HIGHEST)
         if step == 0:
-            row_whole = lax.psum(row_part, "protos")
+            pieces = lax.all_gather(row_part, "protos")
+            row_whole = jnp.sum(pieces, axis=0)
         else:
             row_whole = lax.psum(row_part, "protos")
         row_scale = 1.0 / row_whole

time: 736 us -> 713 us (0.969)
  blocking collectives: 371 us -> 346 us
    psum x3 -> x2, blocking collectives: 173 us -> 115 us  [on_device(): row_whole = lax.psum(row_part, 'protos')]
    all_gather x0 -> x1, blocking collectives: none -> 34.7 us  [on_device(): pieces = lax.all_gather(row_part, 'protos')]
where the time goes in v1:
time: 713 us
  blocking collectives  346 us (49%)
  waiting for transfers between devices  266 us (37%)
  matrix products  66.8 us (9%)
  other arithmetic  14.7 us (2%)
  between operations  14.1 us (2%)
    reduce_scatter x1, waiting for transfers between devices, on_device(): lax.psum_scatter(feature_term, 'protos', scatter_dimension=0, tiled=True)  215 us
    psum x3, blocking collectives, on_device(): col_scale = 1.0 / lax.psum(col_part, 'rows')  118 us
    psum x2, blocking collectives, on_device(): row_whole = lax.psum(row_part, 'protos')  115 us
    reduce_scatter x1, waiting for transfers between devices, on_device(): lax.psum_scatter(term.reshape(row_groups, block, term.shape[1]), 'rows',...  51.2 us
    all_gather x1, blocking collectives, on_device(): lax.all_gather(local_s, 'protos', axis=0, tiled=True)  41.6 us
    all_gather x1, blocking collectives, on_device(): lax.all_gather(local_t, 'protos', axis=0, tiled=True)  36.7 us
    all_gather x1, blocking collectives, on_device(): pieces = lax.all_gather(row_part, 'protos')  34.7 us
    dot_general x3, matrix products, on_device(): row_part = jnp.dot(kernel, col_scale, precision=lax.Precision.HIGHEST)  28.9 us
  transfers between devices with their start and end apart: 2, of which 2 were waited for; matrix products, arithmetic and copies ran while one was open for 1% of the time, Pallas kernels for 0%

profile of v1, /device:TPU:1, one launch (start us, length us, event | category | flops | bytes accessed | tf_op | source)
XLA Modules:
  0.0 712.6 jit_solution(18410232759558618920)
XLA Ops:
  7.2 0.0 reduce-scatter.3.cloned.1.call-start
  7.2 0.8 fusion.5
  8.0 0.8 fusion.3
  8.9 0.8 fusion.4
  9.7 0.8 fusion.6
  10.4 2.6 fusion.1
  13.0 0.0 copy-start.3
  13.1 41.6 %all_gather.12 = bf16[512,384]{1,0:T(8,128)(2,1)S(1)} all-gather(bf16[16,384]{1,0:T(8,128)(2,1)S(1)} %fusion.4), channel_id=1, replica_groups=mesh['rows'=8,'protos'=32] {'protos'}, dimensions={0}, use_global_device_ids=true | all-gather | bytes 405504 | tf_op jit(solution)/shard_map/all_gather | solution.py:33
  54.6 36.7 %all_gather.13 = bf16[512,384]{1,0:T(8,128)(2,1)S(1)} all-gather(bf16[16,384]{1,0:T(8,128)(2,1)S(1)} %fusion.6), channel_id=1, replica_groups=mesh['rows'=8,'protos'=32] {'protos'}, dimensions={0}, use_global_device_ids=true | all-gather | bytes 405504 | tf_op jit(solution)/shard_map/all_gather | solution.py:32
  91.3 4.3 multiply_exponential_fusion
  95.7 0.0 copy-start
  95.7 3.2 copy-done
  98.9 4.0 fusion.7
  102.9 0.0 copy-done.3
  102.9 44.7 %psum.43 = f32[4096]{0:T(1024)S(1)} all-reduce(f32[4096]{0:T(1024)S(1)} %bitcast.37), channel_id=1, replica_groups=mesh['rows'=8,'protos'=32] {'rows'}, use_global_device_ids=true, to_apply=%region_5.0 | all-reduce | flops 4096 | bytes 32768 | tf_op jit(solution)/shard_map/psum | solution.py:43
  147.7 9.4 %convolution_bitcast_fusion = f32[1,1,512]{2,1,0:T(1,128)S(1)} fusion(f32[512,4096]{1,0:T(8,128)} %copy-done, f32[4096,1]{0,1:T(1,128)S(1)} %bitcast.33), kind=kOutput, calls=%fused_computation.10 | convolution fusion | flops 25165824 | bytes 8407040 | tf_op jit(solution)/shard_map/dot_general | solution.py:44
  157.1 34.7 %all-gather.1 = f32[32,1,512]{2,1,0:T(1,128)S(1)} all-gather(f32[1,1,512]{2,1,0:T(1,128)S(1)} %convolution_bitcast_fusion), channel_id=2, replica_groups=mesh['rows'=8,'protos'=32] {'protos'}, dimensions={0}, use_global_device_ids=true | all-gather | bytes 67584 | tf_op jit(solution)/shard_map/all_gather | solution.py:46
  191.8 0.1 reduce_sum.49
  191.9 6.3 fusion.14
  198.3 35.7 %psum.44 = f32[4096]{0:T(1024)S(1)} all-reduce(f32[4096]{0:T(1024)S(1)} %bitcast.34), channel_id=1, replica_groups=mesh['rows'=8,'protos'=32] {'rows'}, use_global_device_ids=true, to_apply=%region_7.0 | all-reduce | flops 4096 | bytes 32768 | tf_op jit(solution)/shard_map/psum | solution.py:43
  233.9 9.4 %fusion.15 = f32[1,512]{1,0:T(1,128)S(1)} fusion(f32[512,4096]{1,0:T(8,128)} %copy-done, f32[4096,1]{0,1:T(1,128)S(1)} %bitcast.35), kind=kOutput, calls=%fused_computation.33 | convolution fusion | flops 25165824 | bytes 8407040 | tf_op jit(solution)/shard_map/dot_general | solution.py:44
  243.4 58.4 %psum.45 = f32[512]{0:T(512)S(1)} all-reduce(f32[512]{0:T(512)S(1)} %bitcast.40), channel_id=1, replica_groups=mesh['rows'=8,'protos'=32] {'protos'}, use_global_device_ids=true, to_apply=%region_8.0 | all-reduce | flops 512 | bytes 4096 | tf_op jit(solution)/shard_map/psum | solution.py:49
  301.8 0.0 copy-start.1
  301.8 6.5 fusion.16
  308.3 37.6 %psum.46 = f32[4096]{0:T(1024)} all-reduce(f32[4096]{0:T(1024)S(1)} %bitcast.36), channel_id=1, replica_groups=mesh['rows'=8,'protos'=32] {'rows'}, use_global_device_ids=true, to_apply=%region_9.0 | all-reduce | flops 4096 | bytes 32768 | tf_op jit(solution)/shard_map/psum | solution.py:43
  345.9 0.7 broadcast_divide_fusion
  346.7 10.0 %fusion.17 = f32[1,512]{1,0:T(1,128)} fusion(f32[512,4096]{1,0:T(8,128)} %copy-done, f32[4096,1]{0,1:T(1,128)S(1)} %bitcast.32), kind=kOutput, calls=%fused_computation.35 | convolution fusion | flops 25165824 | bytes 8407040 | tf_op jit(solution)/shard_map/dot_general | solution.py:44
  356.7 0.0 copy-done.1
  356.7 6.2 fusion
  362.9 56.4 %all-reduce = (f32[512]{0:T(512)}, f32[512]{0:T(512)}) all-reduce(f32[512]{0:T(512)} %bitcast.38, f32[512]{0:T(512)} %get-tuple-element.4), channel_id=1, replica_groups=mesh['rows'=8,'protos'=32] {'protos'}, use_global_device_ids=true, to_apply=%region_10.0 | all-reduce | flops 1024 | bytes 8192 | tf_op jit(solution)/shard_map/psum | solution.py:49
  419.3 0.7 broadcast_divide_fusion.5
  420.0 0.0 copy-start.4
  420.0 7.3 %subtract_convert_fusion = bf16[512,4096]{1,0:T(8,128)(2,1)S(1)} fusion(f32[512,4096]{1,0:T(8,128)} %copy-done, f32[512,4096]{1,0:T(8,128)} %get-tuple-element.5, f32[4096]{0:T(1024)S(1)} %broadcast_divide_fusion, f32[512]{0:T(512)S(1)} %broadcast_divide_fusion.5, f32[512]{0:T(512)} %get-tuple-element.3), kind=kLoop, calls=%fused_computation | loop fusion | flops 12582912 | bytes 20992000 | tf_op jit(solution)/shard_map/convert_element_type | solution.py:53
  427.3 0.0 copy-start.2
  427.3 2.0 copy-done.2
  429.4 0.0 copy-done.4
  429.4 3.3 convolution_multiply_fusion.1
  432.7 0.0 reduce-scatter.3.cloned.1.call-update
  432.7 0.0 reduce-scatter.5.cloned.1.call-start
  432.8 7.2 %convolution_multiply_fusion = f32[4096,384]{1,0:T(8,128)} fusion(bf16[512,4096]{1,0:T(8,128)(2,1)} %copy-done.2, bf16[512,384]{1,0:T(8,128)(2,1)S(1)} %all_gather.12), kind=kOutput, calls=%fused_computation.8 | convolution fusion | flops 1612185600 | bytes 10878976 | tf_op jit(solution)/shard_map/dot_general | solution.py:60
  440.0 0.0 reduce-scatter.5.cloned.1.call-update
  440.0 214.5 %reduce-scatter.3.cloned.1.call-done = f32[16,384]{1,0:T(8,128)} async-done(((f32[512,384]{1,0:T(8,128)}), f32[16,384]{1,0:T(8,128)}) %reduce-scatter.3.cloned.1.call-update) | async-done | bytes 24592 | tf_op jit(solution)/shard_map/reduce_scatter | solution.py:55
  654.6 51.2 %reduce-scatter.5.cloned.1.call-done = f32[1,512,384]{2,1,0:T(8,128)} async-done(((f32[8,512,384]{2,1,0:T(8,128)}), f32[1,512,384]{2,1,0:T(8,128)}) %reduce-scatter.5.cloned.1.call-update) | async-done | bytes 786448 | tf_op jit(solution)/shard_map/reduce_scatter | solution.py:63
  (7 shorter events, 0.0 us)
Async XLA Ops:
  7.2 647.4 %reduce-scatter.3.cloned.1.call-start = ((), (), s32[]{:S(2)}) async-start(), calls=%async_computation.2 | async-start | bytes 811008 | tf_op jit(solution)/shard_map/reduce_scatter | solution.py:55
  13.0 89.9 %copy-start.3 = (f32[4096]{0:T(1024)}, f32[4096]{0:T(1024)S(1)}, u32[]{:S(2)}) copy-start(f32[4096]{0:T(1024)S(1)} %add_rsqrt_fusion) | copy-start | bytes 49156
  95.7 3.2 copy-start
  301.8 54.9 %copy-start.1 = (bf16[4096,384]{1,0:T(8,128)(2,1)S(1)}, bf16[4096,384]{1,0:T(8,128)(2,1)}, u32[]{:S(2)}) copy-start(bf16[4096,384]{1,0:T(8,128)(2,1)} %param.5) | copy-start | bytes 9437188
  420.0 9.4 %copy-start.4 = (f32[4096]{0:T(1024)S(1)}, f32[4096]{0:T(1024)}, u32[]{:S(2)}) copy-start(f32[4096]{0:T(1024)} %copy-done.3) | copy-start | bytes 49156
  427.3 2.0 copy-start.2
  432.7 273.0 %reduce-scatter.5.cloned.1.call-start = ((), (), s32[]{:S(2)}) async-start(), calls=%async_computation.3 | async-start | bytes 7077888 | tf_op jit(solution)/shard_map/reduce_scatter | solution.py:63
Sparse Core Ops, SparseCore 0:
  432.8 221.6 reduce-scatter.2
  657.7 48.0 reduce-scatter.4
